TPU v7x, 128 devices: a whole 4x4x4 slice. The times are simulated.
128 devices in a mesh: row: 8 (over z_hi, y), col: 16 (over z_lo, x, core).
Axes of the slice: x: 4, y: 4, z: 4 (z_hi: 2, z_lo: 2; z = z_hi * 2 + z_lo), core: 2. Of those that a mesh axis runs over, the one named last changes fastest.
Arguments:
- features: bfloat16 [65536, 256], P(('col', 'row')), may hold values from -6 to 6
- weight: bfloat16 [256, 256], replicated, may hold values from -0.375 to 0.375
- bias: float32 [256], replicated, may hold values from -4 to 4
- cotangent: bfloat16 [65536, 256], P(('row', 'col')), may hold values from -6 to 6
- tiles: bfloat16 [8, 16, 384, 128, 128], P('row', 'col'), may hold values from -0.0546875 to 0.0546875
- tile_rows: int32 [8, 16, 384], P('row', 'col'), may hold values from 0 to 63, as said below
- tile_cols: int32 [8, 16, 384], P('row', 'col'), may hold values from 0 to 31
- tile_counts: int32 [8, 16], P('row', 'col'), may hold values from 24 to 384, as said below
Outputs:
- hidden: bfloat16 [65536, 256], P(('row', 'col'))
- grad_weight: float32 [256, 256], replicated
- grad_bias: float32 [256], replicated
- grad_features: bfloat16 [65536, 256], P(('col', 'row'))
Inputs may be any that keep to these rules, and one draw needn't show every extreme that they name: `tile_rows`: on each grid cell the slots name distinct blocks. `tile_counts`: slots at or after a cell's count are unused; some cell uses all 384 slots.
All inputs are finite; a program needn't handle non-finite values.
Results may differ from a plain program's by a relative error of at most 0.013.
Values may be sent and summed in bfloat16 or wider, within the bound.
A program may use at most 128 MiB of HBM per device.

v0:
```python
import math
import jax
import jax.numpy as jnp
from jax import lax
from jax.sharding import PartitionSpec as P


def accumulate(tiles, dest_ids, source_ids, live_count, source_blocks, out_blocks, backward):
    slots = tiles.shape[0]
    group = math.gcd(slots, 32)
    block = tiles.shape[-1]
    width = source_blocks.shape[-1]
    in_blocks = source_blocks.shape[0]
    flat_source = source_blocks.reshape(in_blocks, block * width)
    in_range = jnp.arange(in_blocks, dtype=jnp.int32)
    out_range = jnp.arange(out_blocks, dtype=jnp.int32)

    def one_group(step_index, total):
        start = step_index * group
        tile_group = lax.dynamic_slice_in_dim(tiles, start, group, 0)
        dest_group = lax.dynamic_slice_in_dim(dest_ids, start, group, 0)
        source_group = lax.dynamic_slice_in_dim(source_ids, start, group, 0)
        live = start + jnp.arange(group, dtype=jnp.int32) < live_count
        if backward:
            fetch_ids = dest_group
            target = source_group
        else:
            fetch_ids = source_group
            target = dest_group
        picker = (fetch_ids[:, None] == in_range[None, :]).astype(jnp.bfloat16)
        fetched = jnp.dot(picker, flat_source, preferred_element_type=jnp.float32)
        fetched = fetched.astype(jnp.bfloat16).reshape(group, block, width)
        if backward:
            contrib = jnp.einsum(
                "tji,tjf->tif", tile_group, fetched, preferred_element_type=jnp.float32
            )
        else:
            contrib = jnp.einsum(
                "tij,tjf->tif", tile_group, fetched, preferred_element_type=jnp.float32
            )
        placer = ((target[:, None] == out_range[None, :]) & live[:, None]).astype(jnp.float32)
        added = jnp.dot(
            placer.T,
            contrib.reshape(group, block * width),
            precision=lax.Precision.HIGHEST,
            preferred_element_type=jnp.float32,
        )
        return total + added

    start_total = jnp.zeros((out_blocks, block * width), jnp.float32)
    result = lax.fori_loop(0, slots // group, one_group, start_total)
    return result.reshape(out_blocks, block, width)


def per_device(features, weight, bias, cotangent, tiles, tile_rows, tile_cols, tile_counts):
    tile_set = tiles[0, 0]
    dest_ids = tile_rows[0, 0]
    source_ids = tile_cols[0, 0]
    live_count = tile_counts[0, 0]
    block = tile_set.shape[-1]
    own_nodes = features.shape[0]
    width = features.shape[1]
    row_count = lax.axis_size("row")
    col_count = lax.axis_size("col")
    blocks_down = own_nodes * col_count // block
    blocks_across = own_nodes * row_count // block
    factor = 1.0 / math.sqrt(own_nodes * row_count * col_count)
    panel = lax.all_gather(features, "row", axis=0, tiled=True)
    panel_blocks = panel.reshape(blocks_across, block, width)
    partial_value = accumulate(
        tile_set, dest_ids, source_ids, live_count, panel_blocks, blocks_down, False
    )
    term = partial_value.reshape(blocks_down * block, width)
    summed = lax.psum_scatter(term, "col", scatter_dimension=0, tiled=True)
    aggregated = summed.astype(jnp.bfloat16)
    preact = jnp.dot(aggregated, weight, preferred_element_type=jnp.float32) + bias
    hidden = jax.nn.silu(preact).astype(jnp.bfloat16)
    sigma = jax.nn.sigmoid(preact)
    slope = sigma * (1.0 + preact * (1.0 - sigma))
    grad_pre = (cotangent.astype(jnp.float32) * slope).astype(jnp.bfloat16)
    local_weight = jnp.einsum("nf,ng->fg", aggregated, grad_pre, preferred_element_type=jnp.float32)
    local_bias = jnp.sum(grad_pre.astype(jnp.float32), axis=0)
    grad_agg = jnp.dot(grad_pre, weight.T, preferred_element_type=jnp.float32).astype(jnp.bfloat16)
    grad_panel = lax.all_gather(grad_agg, "col", axis=0, tiled=True)
    grad_blocks = grad_panel.reshape(blocks_down, block, width)
    partial_back = accumulate(
        tile_set, dest_ids, source_ids, live_count, grad_blocks, blocks_across, True
    )
    term_back = partial_back.reshape(blocks_across * block, width)
    grad_features = lax.psum_scatter(
        term_back.astype(jnp.bfloat16), "row", scatter_dimension=0, tiled=True
    )
    grad_weight, grad_bias = lax.psum((local_weight, local_bias), ("row", "col"))
    grad_weight = grad_weight * factor
    grad_bias = grad_bias * factor
    return (hidden, grad_weight, grad_bias, grad_features)


def solution(mesh):
    in_specs = (
        P(("col", "row"), None),
        P(),
        P(),
        P(("row", "col"), None),
        P("row", "col", None, None, None),
        P("row", "col", None),
        P("row", "col", None),
        P("row", "col"),
    )
    out_specs = (P(("row", "col"), None), P(), P(), P(("col", "row"), None))
    return jax.shard_map(
        per_device, mesh=mesh, in_specs=in_specs, out_specs=out_specs, check_vma=False
    )
```

profile of v0, /device:TPU:0, one launch (start us, length us, event | category | flops | bytes accessed | tf_op | source)
XLA Modules:
  0.0 667.1 jit_solution(5247763881698745133)
XLA Ops:
  9.4 58.5 %all-gather.3.cloned.1.call-done = bf16[4096,256]{1,0:T(8,128)(2,1)} async-done(((bf16[512,256]{1,0:T(8,128)(2,1)}), bf16[4096,256]{1,0:T(8,128)(2,1)}) %all-gather.3.cloned.1.call-update) | async-done | bytes 2097168 | tf_op jit(solution)/shard_map/all_gather | solution.py:68
  70.7 196.6 %while.28 = (s32[]{:T(128)}, f32[64,32768]{1,0:T(8,128)}, s32[384]{0:T(512)S(1)}, s32[]{:T(128)}, bf16[384,128,128]{2,1,0:T(8,128)(2,1)}, /*index=5*/s32[384]{0:...) while((s32[]{:T(128)}, f32[64,32768]{1,0:T(8,128)}, ...), condition=%wide.region_1.0_spmd.clone, body=%wide.region_0.0_spmd.clone.sunk | while | flops 1146098688 | bytes 103810120 | solution.py:51
  77.4 6.5 convolution_add_fusion.5
  93.8 6.5 convolution_add_fusion.5
  110.1 6.5 convolution_add_fusion.5
  126.5 6.5 convolution_add_fusion.5
  142.9 6.5 convolution_add_fusion.5
  159.3 6.5 convolution_add_fusion.5
  175.7 6.5 convolution_add_fusion.5
  192.0 6.5 convolution_add_fusion.5
  208.4 6.5 convolution_add_fusion.5
  224.8 6.5 convolution_add_fusion.5
  241.2 6.5 convolution_add_fusion.5
  257.6 6.5 convolution_add_fusion.5
  267.3 9.2 %reshape_reshape.11 = f32[8192,256]{1,0:T(8,128)} reshape(f32[64,32768]{1,0:T(8,128)} %get-tuple-element.312) | data formatting | bytes 16777216 | tf_op jit(solution)/shard_map/reshape;reshape | solution.py:73
  276.6 73.4 %reduce-scatter.3.cloned.1.call-done = f32[512,256]{1,0:T(8,128)} async-done(((f32[8192,256]{1,0:T(8,128)}), f32[512,256]{1,0:T(8,128)}) %reduce-scatter.3.cloned.1.call-update) | async-done | bytes 524304 | tf_op jit(solution)/shard_map/reduce_scatter | solution.py:74
  353.4 16.7 %copy.12 = bf16[1,1,384,128,128]{3,4,2,1,0:T(8,128)(2,1)} copy(bf16[1,1,384,128,128]{4,3,2,1,0:T(8,128)(2,1)} %bitcast.60) | data formatting | bytes 25165824 | tf_op args[4]
  371.2 18.1 %all-gather.5.cloned.1.call-done = bf16[8192,256]{1,0:T(8,128)(2,1)} async-done(((bf16[512,256]{1,0:T(8,128)(2,1)}), bf16[8192,256]{1,0:T(8,128)(2,1)}) %all-gather.5.cloned.1.call-update) | async-done | bytes 4194320 | tf_op jit(solution)/shard_map/all_gather | solution.py:84
  389.2 7.4 %reshape_reshape.12 = bf16[64,32768]{1,0:T(8,128)(2,1)} reshape(bf16[8192,256]{1,0:T(8,128)(2,1)} %all-gather.5.cloned.1.call-done) | data formatting | bytes 8388608 | tf_op jit(solution)/shard_map/reshape;reshape | solution.py:14
  396.6 183.3 %while.29 = (s32[]{:T(128)}, f32[32,32768]{1,0:T(8,128)}, s32[384]{0:T(512)S(1)}, s32[]{:T(128)}, bf16[384,128,128]{1,2,0:T(8,128)(2,1)}, /*index=5*/s32[384]{0:...) while((s32[]{:T(128)}, f32[32,32768]{1,0:T(8,128)}, ...), condition=%wide.region_7.8_spmd.clone, body=%wide.region_6.7_spmd.clone.sunk | while | flops 808456256 | bytes 72352824 | solution.py:51
  481.7 4.7 convolution_add_fusion.6
  496.9 4.7 convolution_add_fusion.6
  573.3 4.7 convolution_add_fusion.6
  584.7 69.3 %psum.15 = f32[256]{0:T(256)S(1)} all-reduce(f32[256]{0:T(256)S(1)} %get-tuple-element.405), channel_id=1, replica_groups=mesh['row'=8,'col'=16] {'row','col'}, use_global_device_ids=true, to_apply=%region_5.6 | all-reduce | flops 256 | bytes 2048 | tf_op jit(solution)/shard_map/psum | solution.py:93
  (343 shorter events, 306.8 us)
Async XLA Ops:
  7.2 342.9 %copy-start = (bf16[256,256]{1,0:T(8,128)(2,1)S(1)}, bf16[256,256]{1,0:T(8,128)(2,1)}, u32[]{:S(2)}) copy-start(bf16[256,256]{1,0:T(8,128)(2,1)} %param.13) | copy-start | bytes 393220
  7.2 60.7 %all-gather.3.cloned.1.call-start = ((), (), s32[]{:S(2)}) async-start(), calls=%async_computation.2 | async-start | bytes 2359296 | tf_op jit(solution)/shard_map/all_gather | solution.py:68
  7.9 342.1 %reduce-scatter.3.cloned.1.call-start = ((), (), s32[]{:S(2)}) async-start(), calls=%async_computation.3 | async-start | bytes 8912896 | tf_op jit(solution)/shard_map/reduce_scatter | solution.py:74
  72.8 4.5 slice-start
  89.2 4.5 slice-start
  100.3 3.2 copy-start.2
  105.6 4.5 slice-start
  116.7 3.2 copy-start.2
  122.0 4.5 slice-start
  138.3 4.5 slice-start
  154.7 4.5 slice-start
  171.1 4.5 slice-start
  187.5 4.5 slice-start
  203.8 4.5 slice-start
  220.2 4.5 slice-start
  236.6 4.5 slice-start
  253.0 4.5 slice-start
  276.6 73.5 %copy-start.6 = (bf16[512,256]{1,0:T(8,128)(2,1)S(1)}, bf16[512,256]{1,0:T(8,128)(2,1)}, u32[]{:S(2)}) copy-start(bf16[512,256]{1,0:T(8,128)(2,1)} %param.15) | copy-start | bytes 786436
  276.6 73.5 %copy-start.7 = (f32[256]{0:T(256)S(1)}, f32[256]{0:T(256)}, u32[]{:S(2)}) copy-start(f32[256]{0:T(256)} %param.14) | copy-start | bytes 3076
  276.6 112.7 %all-gather.5.cloned.1.call-start = ((), (), s32[]{:S(2)}) async-start(), calls=%async_computation.5 | async-start | bytes 4456448 | tf_op jit(solution)/shard_map/all_gather | solution.py:84
  353.2 301.4 %all-reduce.2.cloned.1.call-start = ((), (), s32[]{:S(2)}) async-start(), calls=%async_computation.4 | async-start | bytes 524288 | tf_op jit(solution)/shard_map/psum | solution.py:93
  353.4 16.7 %copy-start.5 = (f32[512,256]{1,0:T(8,128)S(1)}, f32[512,256]{1,0:T(8,128)}, u32[]{:S(2)}) copy-start(f32[512,256]{1,0:T(8,128)} %reduce-scatter.3.cloned.1.call-done) | copy-start | bytes 1572868
  371.1 289.5 %reduce-scatter.5.cloned.1.call-start = ((), (), s32[]{:S(2)}) async-start(), calls=%async_computation.6 | async-start | bytes 2359296 | tf_op jit(solution)/shard_map/reduce_scatter | solution.py:90
  579.9 80.7 %copy-start.1 = (bf16[256,256]{1,0:T(8,128)(2,1)S(1)}, bf16[256,256]{1,0:T(8,128)(2,1)}, u32[]{:S(2)}) copy-start(bf16[256,256]{1,0:T(8,128)(2,1)} %param.13) | copy-start | bytes 393220
  (46 other events, 114.6 us)
Sparse Core Ops, SparseCore 0:
  10.4 57.4 all-gather.2
  276.7 73.2 reduce-scatter.2
  353.3 35.9 all-gather.4
  394.4 141.9 all-reduce.1
  584.8 75.7 reduce-scatter.4
where the time goes:
time: 669 us; the launch traced here: 667 us
  matrix products  231 us (35%)
  local copies, waits for them, and re-layouts  174 us (26%)
  waiting for transfers between devices  155 us (23%)
  blocking collectives  69.3 us (10%)
  other arithmetic  21.7 us (3%)
  between operations  13.8 us (2%)
    dot_general x24, matrix products, one_group(): jnp.dot(placer.T, contrib.reshape(group, block * width), precision=lax.Pr...  134 us
    while x168, local copies, waits for them, and re-layouts  132 us
    reduce_scatter x1, waiting for transfers between devices, per_device(): summed = lax.psum_scatter(term, 'col', scatter_dimension=0, tiled=True)  73.4 us
    psum x1, blocking collectives, per_device(): lax.psum((local_weight, local_bias), ('row', 'col'))  69.3 us
    all_gather x1, waiting for transfers between devices, per_device(): panel = lax.all_gather(features, 'row', axis=0, tiled=True)  58.5 us
    dot_general x24, matrix products, one_group(): fetched = jnp.dot(picker, flat_source, preferred_element_type=jnp.float32)  44.3 us
    dot_general x12, matrix products, one_group(): jnp.einsum('tij,tjf->tif', tile_group, fetched, preferred_element_type=jn...  25 us
    dot_general x12, matrix products, one_group(): jnp.einsum('tji,tjf->tif', tile_group, fetched, preferred_element_type=jn...  23.2 us
  transfers between devices with their start and end apart: 5, of which 4 were waited for; matrix products, arithmetic and copies ran while one was open for 29% of the time, Pallas kernels for 0%

commit v1 on v0

--- a/solution.py
+++ b/solution.py
@@ -81,7 +81,9 @@
     local_weight = jnp.einsum("nf,ng->fg", aggregated, grad_pre, preferred_element_type=jnp.float32)
     local_bias = jnp.sum(grad_pre.astype(jnp.float32), axis=0)
     grad_agg = jnp.dot(grad_pre, weight.T, preferred_element_type=jnp.float32).astype(jnp.bfloat16)
-    grad_panel = lax.all_gather(grad_agg, "col", axis=0, tiled=True)
+    grad_panel = jnp.concatenate(
+        lax.all_to_all(jnp.stack([grad_agg] * lax.axis_size("col")), "col", 0, 0), axis=0
+    )
     grad_blocks = grad_panel.reshape(blocks_down, block, width)
     partial_back = accumulate(
         tile_set, dest_ids, source_ids, live_count, grad_blocks, blocks_across, True

time: 669 us -> 697 us (1.042)
  waiting for transfers between devices: 155 us -> 176 us
    all_to_all x0 -> x1, waiting for transfers between devices: none -> 38.6 us  [per_device(): lax.all_to_all(jnp.stack([grad_agg] * lax.axis_size('col')), 'col', 0, 0)]
    all_gather x1 -> x0, waiting for transfers between devices: 18.1 us -> none  [per_device(): grad_panel = lax.all_gather(grad_agg, 'col', axis=0, tiled=True)]
  transfers between devices with their start and end apart: 5 -> 5, of which waited for: 4 -> 4; matrix products, arithmetic and copies ran while one was open for 29% -> 28% of each run, Pallas kernels for 0% -> 0%
where the time goes in v1:
time: 697 us; the launch traced here: 694 us
  matrix products  230 us (33%)
  local copies, waits for them, and re-layouts  177 us (25%)
  waiting for transfers between devices  176 us (25%)
  blocking collectives  70.1 us (10%)
  other arithmetic  21.7 us (3%)
  between operations  13.8 us (2%)
    dot_general x24, matrix products, one_group(): jnp.dot(placer.T, contrib.reshape(group, block * width), precision=lax.Pr...  134 us
    while x168, local copies, waits for them, and re-layouts  132 us
    reduce_scatter x1, waiting for transfers between devices, per_device(): summed = lax.psum_scatter(term, 'col', scatter_dimension=0, tiled=True)  73.4 us
    psum x1, blocking collectives, per_device(): lax.psum((local_weight, local_bias), ('row', 'col'))  70.1 us
    all_gather x1, waiting for transfers between devices, per_device(): panel = lax.all_gather(features, 'row', axis=0, tiled=True)  58.5 us
    dot_general x24, matrix products, one_group(): fetched = jnp.dot(picker, flat_source, preferred_element_type=jnp.float32)  44.4 us
    all_to_all x1, waiting for transfers between devices, per_device(): lax.all_to_all(jnp.stack([grad_agg] * lax.axis_size('col')), 'col', 0, 0)  38.6 us
    dot_general x12, matrix products, one_group(): jnp.einsum('tij,tjf->tif', tile_group, fetched, preferred_element_type=jn...  25 us
  transfers between devices with their start and end apart: 5, of which 4 were waited for; matrix products, arithmetic and copies ran while one was open for 28% of the time, Pallas kernels for 0%

profile of v1, /device:TPU:0, one launch (start us, length us, event | category | flops | bytes accessed | tf_op | source)
XLA Modules:
  0.0 694.5 jit_solution(3252629322665225685)
XLA Ops:
  9.4 58.5 %all-gather.2.cloned.1.call-done = bf16[4096,256]{1,0:T(8,128)(2,1)} async-done(((bf16[512,256]{1,0:T(8,128)(2,1)}), bf16[4096,256]{1,0:T(8,128)(2,1)}) %all-gather.2.cloned.1.call-update) | async-done | bytes 2097168 | tf_op jit(solution)/shard_map/all_gather | solution.py:68
  70.7 196.7 %while.28 = (s32[]{:T(128)}, f32[64,32768]{1,0:T(8,128)}, s32[384]{0:T(512)S(1)}, s32[]{:T(128)}, bf16[384,128,128]{2,1,0:T(8,128)(2,1)}, /*index=5*/s32[384]{0:...) while((s32[]{:T(128)}, f32[64,32768]{1,0:T(8,128)}, ...), condition=%wide.region_1.0_spmd.clone, body=%wide.region_0.0_spmd.clone.sunk | while | flops 1146098688 | bytes 103810120 | solution.py:51
  77.4 6.5 convolution_add_fusion.5
  93.8 6.5 convolution_add_fusion.5
  110.2 6.5 convolution_add_fusion.5
  126.6 6.5 convolution_add_fusion.5
  143.0 6.5 convolution_add_fusion.5
  159.4 6.5 convolution_add_fusion.5
  175.7 6.5 convolution_add_fusion.5
  192.1 6.5 convolution_add_fusion.5
  208.5 6.5 convolution_add_fusion.5
  224.9 6.5 convolution_add_fusion.5
  241.3 6.5 convolution_add_fusion.5
  257.7 6.5 convolution_add_fusion.5
  267.4 9.2 %reshape_reshape.8 = f32[8192,256]{1,0:T(8,128)} reshape(f32[64,32768]{1,0:T(8,128)} %get-tuple-element.312) | data formatting | bytes 16777216 | tf_op jit(solution)/shard_map/reshape;reshape | solution.py:73
  276.7 73.4 %reduce-scatter.3.cloned.1.call-done = f32[512,256]{1,0:T(8,128)} async-done(((f32[8192,256]{1,0:T(8,128)}), f32[512,256]{1,0:T(8,128)}) %reduce-scatter.3.cloned.1.call-update) | async-done | bytes 524304 | tf_op jit(solution)/shard_map/reduce_scatter | solution.py:74
  354.9 4.7 all-to-all-start
  359.7 16.7 %copy.12 = bf16[1,1,384,128,128]{3,4,2,1,0:T(8,128)(2,1)} copy(bf16[1,1,384,128,128]{4,3,2,1,0:T(8,128)(2,1)} %bitcast.60) | data formatting | bytes 25165824 | tf_op args[4]
  377.4 38.6 %all-to-all-done = bf16[16,512,256]{2,1,0:T(8,128)(2,1)} async-done(((bf16[16,512,256]{2,1,0:T(8,128)(2,1)}), bf16[16,512,256]{2,1,0:T(8,128)(2,1)}, u32[]{:S(2)}, u32[]{:S(2)}) %all-to-all-start) | async-done | bytes 4194336 | tf_op jit(solution)/shard_map/all_to_all | solution.py:85
  416.0 7.4 %reshape_reshape_reshape.3 = bf16[64,32768]{1,0:T(8,128)(2,1)} reshape(bf16[16,512,256]{2,1,0:T(8,128)(2,1)} %all-to-all-done) | data formatting | bytes 8388608 | tf_op jit(solution)/shard_map/reshape;reshape;reshape | solution.py:14
  423.4 183.1 %while.29 = (s32[]{:T(128)}, f32[32,32768]{1,0:T(8,128)}, s32[384]{0:T(512)S(1)}, s32[]{:T(128)}, bf16[384,128,128]{1,2,0:T(8,128)(2,1)}, /*index=5*/s32[384]{0:...) while((s32[]{:T(128)}, f32[32,32768]{1,0:T(8,128)}, ...), condition=%wide.region_7.8_spmd.clone, body=%wide.region_6.7_spmd.clone.sunk | while | flops 808456256 | bytes 72352824 | solution.py:51
  432.1 4.7 convolution_add_fusion.6
  493.1 4.7 convolution_add_fusion.6
  611.3 70.1 %psum.15 = f32[256]{0:T(256)S(1)} all-reduce(f32[256]{0:T(256)S(1)} %get-tuple-element.405), channel_id=1, replica_groups=mesh['row'=8,'col'=16] {'row','col'}, use_global_device_ids=true, to_apply=%region_5.6 | all-reduce | flops 256 | bytes 2048 | tf_op jit(solution)/shard_map/psum | solution.py:95
  (343 shorter events, 312.8 us)
Async XLA Ops:
  7.2 343.0 %copy-start = (bf16[256,256]{1,0:T(8,128)(2,1)S(1)}, bf16[256,256]{1,0:T(8,128)(2,1)}, u32[]{:S(2)}) copy-start(bf16[256,256]{1,0:T(8,128)(2,1)} %param.13) | copy-start | bytes 393220
  7.2 60.7 %all-gather.2.cloned.1.call-start = ((), (), s32[]{:S(2)}) async-start(), calls=%async_computation.3 | async-start | bytes 2359296 | tf_op jit(solution)/shard_map/all_gather | solution.py:68
  7.9 342.2 %reduce-scatter.3.cloned.1.call-start = ((), (), s32[]{:S(2)}) async-start(), calls=%async_computation.4 | async-start | bytes 8912896 | tf_op jit(solution)/shard_map/reduce_scatter | solution.py:74
  72.8 4.5 slice-start
  83.9 3.2 copy-start.2
  89.2 4.5 slice-start
  100.3 3.2 copy-start.2
  105.6 4.5 slice-start
  122.0 4.5 slice-start
  138.4 4.5 slice-start
  154.8 4.5 slice-start
  171.2 4.5 slice-start
  187.6 4.5 slice-start
  204.0 4.5 slice-start
  220.3 4.5 slice-start
  236.7 4.5 slice-start
  253.1 4.5 slice-start
  276.7 73.5 %copy-start.6 = (bf16[512,256]{1,0:T(8,128)(2,1)S(1)}, bf16[512,256]{1,0:T(8,128)(2,1)}, u32[]{:S(2)}) copy-start(bf16[512,256]{1,0:T(8,128)(2,1)} %param.15) | copy-start | bytes 786436
  276.7 73.5 %copy-start.7 = (f32[256]{0:T(256)S(1)}, f32[256]{0:T(256)}, u32[]{:S(2)}) copy-start(f32[256]{0:T(256)} %param.14) | copy-start | bytes 3076
  354.9 61.1 %all-to-all-start = ((bf16[16,512,256]{2,1,0:T(8,128)(2,1)}), bf16[16,512,256]{2,1,0:T(8,128)(2,1)}, u32[]{:S(2)}, u32[]{:S(2)}) async-start(bf16[16,512,256]{2,1,0:T(8,128)(2,1)} %stack.2), calls=%async_computation.1 | async-start | bytes 8388608 | tf_op jit(solution)/shard_map/all_to_all | solution.py:85
  359.6 322.3 %all-reduce.2.cloned.1.call-start = ((), (), s32[]{:S(2)}) async-start(), calls=%async_computation.5 | async-start | bytes 524288 | tf_op jit(solution)/shard_map/psum | solution.py:95
  359.7 16.7 %copy-start.5 = (f32[512,256]{1,0:T(8,128)S(1)}, f32[512,256]{1,0:T(8,128)}, u32[]{:S(2)}) copy-start(f32[512,256]{1,0:T(8,128)} %reduce-scatter.3.cloned.1.call-done) | copy-start | bytes 1572868
  377.4 310.5 %reduce-scatter.5.cloned.1.call-start = ((), (), s32[]{:S(2)}) async-start(), calls=%async_computation.6 | async-start | bytes 2359296 | tf_op jit(solution)/shard_map/reduce_scatter | solution.py:92
  606.5 81.4 %copy-start.1 = (bf16[256,256]{1,0:T(8,128)(2,1)S(1)}, bf16[256,256]{1,0:T(8,128)(2,1)}, u32[]{:S(2)}) copy-start(bf16[256,256]{1,0:T(8,128)(2,1)} %param.13) | copy-start | bytes 393220
  (46 other events, 114.5 us)
Sparse Core Ops, SparseCore 0:
  10.3 57.4 all-gather.1
  276.8 73.2 reduce-scatter.2
  377.5 159.8 all-reduce.1
  611.5 76.4 reduce-scatter.4
